TPU v7x, 32 devices: a whole 2x2x4 slice. The times are simulated.
32 devices in a mesh: grp: 4 (over x, core), var: 8 (over z, y).
Axes of the slice: x: 2, y: 2, z: 4, core: 2. Of those that a mesh axis runs over, the one named last changes fastest.
Arguments:
- dosages: int32 [16384, 8192], P('grp', 'var'), may hold values from 0 to 2
- variant_weight: bfloat16 [8192], P('var'), may hold values from -2 to 2
- block_id: int32 [8192], P('var'), may hold values from 0 to 127
- stack_weight: bfloat16 [1024, 64], replicated, may hold values from -0.1875 to 0.1875
- labels: int32 [16384, 64], P(('grp', 'var')), may hold values 0 or 1
Outputs:
- level_grad: float32 [1024, 64], P('var')
- weight_grad: float32 [8192], P('var')
All inputs are finite; a program needn't handle non-finite values. No bound on the sum of `labels` on one device may be relied on, other than what follows from the above.
Results may differ from a plain program's by a relative error of at most 0.00039.
Values may be sent and summed in bfloat16 or wider, within the bound.
A program may use at most 64 MiB of HBM per device.

v0:
```python
import math

import jax
import jax.numpy as jnp
from jax import lax
from jax.sharding import PartitionSpec as P


def owned_level(predictors, group_resid, norm_scale):
    owned = (
        lax.dot_general(
            predictors, group_resid, (((0,), (0,)), ((), ())), preferred_element_type=jnp.float32
        )
        * norm_scale
    )
    return lax.psum(owned, "grp")


def local(dosages, variant_weight, block_id, stack_weight, labels):
    person_rows = dosages.shape[0]
    total_preds = stack_weight.shape[0]
    var_count = lax.axis_size("var")
    per_device = total_preds // var_count
    norm_scale = 1.0 / math.sqrt(person_rows * lax.axis_size("grp"))
    dose_vals = dosages.astype(jnp.bfloat16)
    one_hot = block_id[:, None] == lax.iota(jnp.int32, per_device)[None, :]
    weighted = jnp.where(one_hot, variant_weight[:, None], jnp.zeros((), jnp.bfloat16))
    predictors = jnp.dot(dose_vals, weighted, preferred_element_type=jnp.float32).astype(
        jnp.bfloat16
    )
    regrouped = None
    regrouped = lax.all_to_all(predictors, "var", split_axis=0, concat_axis=1, tiled=True)
    logits = jnp.dot(regrouped, stack_weight, preferred_element_type=jnp.float32)
    resid = (jax.nn.sigmoid(logits) - labels.astype(jnp.float32)).astype(jnp.bfloat16)
    group_resid = None
    group_resid = lax.all_gather(resid, "var", axis=0, tiled=True)
    level_grad = owned_level(predictors, group_resid, norm_scale)
    full_grad = lax.dot_general(
        resid, stack_weight, (((1,), (1,)), ((), ())), preferred_element_type=jnp.float32
    ).astype(jnp.bfloat16)
    local_grad = lax.all_to_all(full_grad, "var", split_axis=1, concat_axis=0, tiled=True)
    column_grad = lax.dot_general(
        dose_vals, local_grad, (((0,), (0,)), ((), ())), preferred_element_type=jnp.float32
    )
    local_weight = jnp.sum(jnp.where(one_hot, column_grad, 0.0), axis=1) * norm_scale
    weight_grad = lax.psum(local_weight, "grp")
    return (level_grad, weight_grad)


def solution(mesh):
    return jax.shard_map(
        local,
        mesh=mesh,
        in_specs=(P("grp", "var"), P("var"), P("var"), P(), P(("grp", "var"), None)),
        out_specs=(P("var", None), P("var")),
        check_vma=False,
    )
```

profile of v0, /device:TPU:0, one launch (start us, length us, event | category | flops | bytes accessed | tf_op | source)
XLA Modules:
  0.0 113.5 jit_solution(6263934042086971203)
XLA Ops:
  0.6 0.0 copy-start
  0.6 0.0 copy-start.2
  0.7 8.8 %convolution_convert_fusion = bf16[128,4096]{1,0:T(8,128)(2,1)S(1)} fusion(s32[4096,1024]{1,0:T(8,128)} %param.5, s32[1024]{0:T(1024)} %param.7, bf16[1024]{0:T(1024)(128)(2,1)} %param.6), kind=kOutput, calls=%fused_computation | convolution fusion | flops 1078722560 | bytes 17831936 | tf_op jit(solution)/shard_map/dot_general | solution.py:28
  9.4 0.0 copy-start.1
  9.4 0.1 copy.14
  9.5 32.9 %all_to_all.38 = bf16[8,512,128]{1,2,0:T(8,128)(2,1)S(1)} all-to-all(bf16[8,512,128]{1,2,0:T(8,128)(2,1)S(1)} %bitcast.31), channel_id=1, replica_groups=mesh['grp'=4,'var'=8] {'var'}, dimensions={0} | all-to-all | bytes 2097152 | tf_op jit(solution)/shard_map/all_to_all | solution.py:32
  42.4 0.0 copy-done
  42.4 0.0 copy-done.2
  42.4 0.3 fusion.17
  42.8 0.4 fusion.3
  43.2 1.2 %copy.13 = bf16[64,8,8,128]{3,2,0,1:T(8,128)(2,1)} copy(bf16[64,8,8,128]{3,2,1,0:T(8,128)(2,1)S(1)} %fusion.3) | data formatting | bytes 2097152 | tf_op jit(solution)/shard_map/all_to_all | solution.py:41
  44.4 3.6 %all-to-all-start.1 = ((bf16[512,8,128]{2,0,1:T(8,128)(2,1)}), bf16[512,8,128]{2,0,1:T(8,128)(2,1)S(1)}, u32[]{:S(2)}, u32[]{:S(2)}) async-start(bf16[512,8,128]{2,0,1:T(8,128)(2,1)} %bitcast.27), calls=%async_computation.1 | async-start | bytes 2097152 | tf_op jit(solution)/shard_map/all_to_all | solution.py:41
  48.0 46.9 %all_gather.3 = bf16[4096,64]{0,1:T(8,128)(2,1)S(1)} all-gather(bf16[512,64]{0,1:T(8,128)(2,1)S(1)} %fusion.17), channel_id=1, replica_groups=mesh['grp'=4,'var'=8] {'var'}, dimensions={0}, use_global_device_ids=true | all-gather | bytes 589824 | tf_op jit(solution)/shard_map/all_gather | solution.py:36
  94.9 0.5 convolution_multiply_fusion
  95.4 0.0 all-to-all-done.1
  95.4 0.0 copy-done.1
  95.4 7.1 %fusion.10 = f32[1024]{0:T(1024)S(1)} fusion(bf16[4096,128]{1,0:T(8,128)(2,1)S(1)} %bitcast.30, s32[4096,1024]{1,0:T(8,128)} %param.5, s32[1024]{0:T(1024)S(1)} %copy-done.1), kind=kOutput, calls=%fused_computation.8 | convolution fusion | flops 1078328320 | bytes 17833984 | tf_op jit(solution)/shard_map/dot_general | solution.py:42
  102.5 11.1 %all-reduce = (f32[128,64]{0,1:T(8,128)}, f32[1024]{0:T(1024)}) all-reduce(f32[128,64]{0,1:T(8,128)S(1)} %convolution_multiply_fusion, f32[1024]{0:T(1024)S(1)} %broadcast_multiply_fusion), channel_id=1, replica_groups=mesh['grp'=4,'var'=8] {'grp'}, use_global_device_ids=true, to_apply=%region_0.1 | all-reduce | flops 9216 | bytes 73728 | tf_op jit(solution)/shard_map/psum | solution.py:16
  (1 shorter events, 0.0 us)
Async XLA Ops:
  0.6 41.8 %copy-start = (bf16[1024,64]{0,1:T(8,128)(2,1)S(1)}, bf16[1024,64]{0,1:T(8,128)(2,1)}, u32[]{:S(2)}) copy-start(bf16[1024,64]{0,1:T(8,128)(2,1)} %param.8) | copy-start | bytes 393220
  0.6 41.8 %copy-start.2 = (s32[512,64]{0,1:T(8,128)S(1)}, s32[512,64]{0,1:T(8,128)}, u32[]{:S(2)}) copy-start(s32[512,64]{0,1:T(8,128)} %param.9) | copy-start | bytes 393220
  9.4 86.0 %copy-start.1 = (s32[1024]{0:T(1024)S(1)}, s32[1024]{0:T(1024)}, u32[]{:S(2)}) copy-start(s32[1024]{0:T(1024)} %param.7) | copy-start | bytes 12292
  44.4 51.0 %all-to-all-start.1 = ((bf16[512,8,128]{2,0,1:T(8,128)(2,1)}), bf16[512,8,128]{2,0,1:T(8,128)(2,1)S(1)}, u32[]{:S(2)}, u32[]{:S(2)}) async-start(bf16[512,8,128]{2,0,1:T(8,128)(2,1)} %bitcast.27), calls=%async_computation.1 | async-start | bytes 2097152 | tf_op jit(solution)/shard_map/all_to_all | solution.py:41
where the time goes:
time: 114 us
  blocking collectives  90.8 us (80%)
  matrix products  17.1 us (15%)
  starting transfers between devices  3.6 us (3%)
  local copies, waits for them, and re-layouts  1.29 us (1%)
    all_gather x1, blocking collectives, local(): group_resid = lax.all_gather(resid, 'var', axis=0, tiled=True)  46.9 us
    all_to_all x1, blocking collectives, local(): lax.all_to_all(predictors, 'var', split_axis=0, concat_axis=1, tiled=True)  32.9 us
    psum x1, blocking collectives, owned_level(): return lax.psum(owned, 'grp')  11.1 us
    dot_general x1, matrix products, local(): jnp.dot(dose_vals, weighted, preferred_element_type=jnp.float32)  8.76 us
    dot_general x1, matrix products, local(): lax.dot_general(dose_vals, local_grad, (((0,), (0,)), ((), ())), preferre...  7.06 us
    all_to_all x1, starting transfers between devices, local(): lax.all_to_all(full_grad, 'var', split_axis=1, concat_axis=0, tiled=True)  3.6 us
  transfers between devices with their start and end apart: 1, of which 0 were waited for; matrix products, arithmetic and copies ran while one was open for 0% of the time, Pallas kernels for 0%

commit v1 on v0

v1 whole, which is shorter than its diff:
```python
import functools
import math

import jax
import jax.numpy as jnp
from jax import lax
from jax.experimental import pallas as pl
from jax.experimental.pallas import tpu as pltpu
from jax.sharding import PartitionSpec as P

F32, BF16 = jnp.float32, jnp.bfloat16


def flip(a, k, count):
    total, bit = 0, 1
    while bit < count:
        total = total + bit * ((a // bit + k // bit) % 2)
        bit *= 2
    return total


def kernel(
    nvar, ngrp, norm, dos, wt, bid, sw, lab, lev_out, wg_out,
    dint, dose, wmat, bd, wown, labv, pred, part, own, yrecv, ysum, zrecv, gathz, gathy,
    colacc, levacc, redl, redw,
    dsem, csem, ys, yr, zs, zr, gzs, gzr, gys, gyr, rs, rr,
):
    nz = nvar // 2
    rows = labv.shape[0]
    half = rows // 2
    kb, traits = wown.shape
    v = lax.axis_index("var")
    g = lax.axis_index("grp")
    z, y = v // 2, v % 2
    partner = z * 2 + (1 - y)

    def block_of(i, parity):
        return flip(z, nz - 1 - i, nz) * 2 + parity

    def dose_copy(s, b):
        start = pl.multiple_of(b * rows, rows)
        return pltpu.make_async_copy(dos.at[pl.ds(start, rows)], dint.at[s], dsem.at[s])

    sw_copy = pltpu.make_async_copy(sw.at[pl.ds(pl.multiple_of(v * kb, kb), kb)], wown, csem.at[0])
    lab_copy = pltpu.make_async_copy(lab, labv, csem.at[1])
    sw_copy.start()
    for i in range(nz):
        dose_copy(i, block_of(i, 1 - y)).start()
    for i in range(nz):
        dose_copy(nz + i, block_of(i, y)).start()
    lab_copy.start()

    barrier = pltpu.get_barrier_semaphore()
    pl.semaphore_signal(barrier, inc=1, device_id={"var": partner})
    for i in range(nz - 1):
        pl.semaphore_signal(barrier, inc=1, device_id={"var": block_of(i, y)})
    for d in range(1, ngrp):
        pl.semaphore_signal(barrier, inc=1, device_id={"grp": (g + d) % ngrp})

    hot = lax.broadcasted_iota(jnp.int32, (kb, wt.shape[1]), 0) == bid[...]
    wmat[...] = jnp.where(hot, wt[...].astype(F32), 0.0).T.astype(BF16)
    sw_copy.wait()
    w = wown[...].astype(F32)
    zero = jnp.zeros_like(w)
    bd[0:kb, :] = jnp.concatenate([w, zero], axis=1).astype(BF16)
    bd[kb : 2 * kb, :] = jnp.concatenate([zero, w], axis=1).astype(BF16)
    colacc[...] = jnp.zeros_like(colacc)
    levacc[...] = jnp.zeros_like(levacc)

    def forward(s, b):
        dose_copy(s, b).wait()
        d = dint[s].astype(F32).astype(BF16)
        dose[b] = d
        p = jnp.dot(d, wmat[...], preferred_element_type=F32).astype(BF16)
        pp = jnp.concatenate([p[:half], p[half:]], axis=1)
        pred[b] = pp
        return jnp.dot(pp, bd[...], preferred_element_type=F32)

    def y_copy(i):
        return pltpu.make_async_remote_copy(
            part.at[i], yrecv.at[i], ys.at[i], yr.at[i], device_id={"var": partner}
        )

    def z_copy(i):
        return pltpu.make_async_remote_copy(
            ysum.at[i], zrecv.at[i], zs.at[i], zr.at[i], device_id={"var": block_of(i, y)}
        )

    def gz_copy(i):
        return pltpu.make_async_remote_copy(
            gathz.at[nz - 1], gathz.at[i], gzs.at[i], gzr.at[i], device_id={"var": block_of(i, y)}
        )

    def gy_copy(i):
        return pltpu.make_async_remote_copy(
            gathz.at[i], gathy.at[i], gys.at[i], gyr.at[i], device_id={"var": partner}
        )

    part[0] = forward(0, block_of(0, 1 - y))
    pl.semaphore_wait(barrier, nz + ngrp - 1)
    y_copy(0).start()

    def first(i, carry):
        part[i] = forward(i, block_of(i, 1 - y))
        y_copy(i).start()
        return carry

    lax.fori_loop(1, nz, first, 0)

    def second(i, carry):
        own[i] = forward(nz + i, block_of(i, y))
        return carry

    lax.fori_loop(0, nz, second, 0)

    lab_copy.wait()
    target = labv[...].astype(F32)
    target = jnp.concatenate([target[:half], target[half:]], axis=1)

    for i in range(nz - 1):
        y_copy(i).wait_recv()
        ysum[i] = own[i] + yrecv[i]
        z_copy(i).start()
    y_copy(nz - 1).wait_recv()
    logits = own[nz - 1] + yrecv[nz - 1]
    for i in range(nz - 1):
        z_copy(i).wait_recv()
        logits = logits + zrecv[i]
    gathz[nz - 1] = (jax.nn.sigmoid(logits) - target).astype(BF16)
    for i in range(nz - 1):
        gz_copy(i).start()
    gy_copy(nz - 1).start()

    def backward(resid, b):
        lg = lax.dot_general(
            resid, bd[...], (((1,), (1,)), ((), ())), preferred_element_type=F32
        ).astype(BF16)
        lg = jnp.concatenate([lg[:, :kb], lg[:, kb:]], axis=0)
        colacc[...] += lax.dot_general(
            lg, dose[b], (((0,), (0,)), ((), ())), preferred_element_type=F32
        )
        levacc[...] += lax.dot_general(
            pred[b], resid, (((0,), (0,)), ((), ())), preferred_element_type=F32
        )

    backward(gathz[nz - 1], v)
    gy_copy(nz - 1).wait_recv()
    backward(gathy[nz - 1], partner)

    def gather_z(i, carry):
        gz_copy(i).wait_recv()
        gy_copy(i).start()
        backward(gathz[i], block_of(i, y))
        return carry

    lax.fori_loop(0, nz - 1, gather_z, 0)

    def gather_y(i, carry):
        gy_copy(i).wait_recv()
        backward(gathy[i], block_of(i, 1 - y))
        return carry

    lax.fori_loop(0, nz - 1, gather_y, 0)

    hot = lax.broadcasted_iota(jnp.int32, colacc.shape, 0) == bid[...]
    redw[g] = jnp.sum(jnp.where(hot, colacc[...], 0.0), axis=0, keepdims=True)
    lev = levacc[0:kb, 0:traits] + levacc[kb : 2 * kb, traits : 2 * traits]
    redl[g] = jnp.concatenate([lev[: kb // 2], lev[kb // 2 :]], axis=1)

    def r_copies(d):
        peer = {"grp": (g + d) % ngrp}
        return (
            pltpu.make_async_remote_copy(
                redl.at[g], redl.at[g], rs.at[0, d - 1], rr.at[0, d - 1], device_id=peer
            ),
            pltpu.make_async_remote_copy(
                redw.at[g], redw.at[g], rs.at[1, d - 1], rr.at[1, d - 1], device_id=peer
            ),
        )

    for d in range(1, ngrp):
        for copy in r_copies(d):
            copy.start()
    for d in range(1, ngrp):
        for copy in r_copies(d):
            copy.wait_recv()
    total, weight = redl[0], redw[0]
    for e in range(1, ngrp):
        total = total + redl[e]
        weight = weight + redw[e]
    total = total * norm
    lev_out[0 : kb // 2, :] = total[:, :traits]
    lev_out[kb // 2 : kb, :] = total[:, traits:]
    wg_out[...] = weight * norm

    for i in range(nz):
        y_copy(i).wait_send()
        gy_copy(i).wait_send()
    for i in range(nz - 1):
        z_copy(i).wait_send()
        gz_copy(i).wait_send()
    for d in range(1, ngrp):
        for copy in r_copies(d):
            copy.wait_send()


def local(dosages, variant_weight, block_id, stack_weight, labels):
    persons, variants = dosages.shape
    nvar, ngrp = lax.axis_size("var"), lax.axis_size("grp")
    total_preds, traits = stack_weight.shape
    kb = total_preds // nvar
    rows = labels.shape[0]
    half, nz = rows // 2, nvar // 2
    norm = 1.0 / math.sqrt(persons * ngrp)
    block = (half, 2 * traits)
    dma = pltpu.SemaphoreType.DMA
    hbm = pl.BlockSpec(memory_space=pl.ANY)
    vmem = pl.BlockSpec(memory_space=pltpu.VMEM)
    level, weight = pl.pallas_call(
        functools.partial(kernel, nvar, ngrp, norm),
        out_shape=(
            jax.ShapeDtypeStruct((kb, traits), F32),
            jax.ShapeDtypeStruct((1, variants), F32),
        ),
        in_specs=[hbm, vmem, vmem, hbm, hbm],
        out_specs=(vmem, vmem),
        scratch_shapes=[
            pltpu.VMEM((nvar, rows, variants), jnp.int32),
            pltpu.VMEM((nvar, rows, variants), BF16),
            pltpu.VMEM((variants, kb), BF16),
            pltpu.VMEM((2 * kb, 2 * traits), BF16),
            pltpu.VMEM((kb, traits), BF16),
            pltpu.VMEM((rows, traits), jnp.int32),
            pltpu.VMEM((nvar, half, 2 * kb), BF16),
            pltpu.VMEM((nz,) + block, F32),
            pltpu.VMEM((nz,) + block, F32),
            pltpu.VMEM((nz,) + block, F32),
            pltpu.VMEM((nz,) + block, F32),
            pltpu.VMEM((nz,) + block, F32),
            pltpu.VMEM((nz,) + block, BF16),
            pltpu.VMEM((nz,) + block, BF16),
            pltpu.VMEM((kb, variants), F32),
            pltpu.VMEM((2 * kb, 2 * traits), F32),
            pltpu.VMEM((ngrp, kb // 2, 2 * traits), F32),
            pltpu.VMEM((ngrp, 1, variants), F32),
            dma((nvar,)),
            dma((2,)),
            dma((nz,)),
            dma((nz,)),
            dma((nz,)),
            dma((nz,)),
            dma((nz,)),
            dma((nz,)),
            dma((nz,)),
            dma((nz,)),
            dma((2, ngrp - 1)),
            dma((2, ngrp - 1)),
        ],
        compiler_params=pltpu.CompilerParams(
            collective_id=0, has_side_effects=True, vmem_limit_bytes=60 * 1024 * 1024
        ),
    )(dosages, variant_weight[None, :], block_id[None, :], stack_weight, labels)
    return level, weight.reshape(variants)


def solution(mesh):
    return jax.shard_map(
        local,
        mesh=mesh,
        in_specs=(P("grp", "var"), P("var"), P("var"), P(), P(("grp", "var"), None)),
        out_specs=(P("var", None), P("var")),
        check_vma=False,
    )
```

time: 114 us -> 50 us (0.44)
  blocking collectives: 90.8 us -> 0 us
  Pallas kernels: 0 us -> 41.5 us
  matrix products: 17.1 us -> 0 us
  local copies, waits for them, and re-layouts: 1.29 us -> 7.55 us
  starting transfers between devices: 3.6 us -> 0 us
    all_gather x1 -> x0, blocking collectives: 46.9 us -> none  [local(): group_resid = lax.all_gather(resid, 'var', axis=0, tiled=True)]
    pallas_call x0 -> x1, Pallas kernels: none -> 41.5 us  [local(): pl.pallas_call(functools.partial(kernel, nvar, ngrp, norm), out_shape=(ja...]
    all_to_all x1 -> x0, blocking collectives: 32.9 us -> none  [local(): lax.all_to_all(predictors, 'var', split_axis=0, concat_axis=1, tiled=True)]
    dot_general x5 -> x0, matrix products: 17.1 us -> none  [the longest x1 8.76 us: local(): jnp.dot(dose_vals, weighted, preferred_element_type=jnp.float32)]
    psum x1 -> x0, blocking collectives: 11.1 us -> none  [owned_level(): return lax.psum(owned, 'grp')]
    unnamed x6 -> x4, local copies, waits for them, and re-layouts: 0.02 us -> 6.27 us
    all_to_all x1 -> x0, starting transfers between devices: 3.6 us -> none  [local(): lax.all_to_all(full_grad, 'var', split_axis=1, concat_axis=0, tiled=True)]
    broadcast_in_dim x0 -> x1, local copies, waits for them, and re-layouts: none -> 1.28 us  [local(): variant_weight[None, :]]
  transfers between devices with their start and end apart: 1 -> 0, of which waited for: 0 -> 0; matrix products, arithmetic and copies ran while one was open for 0% -> 0% of each run, Pallas kernels for 0% -> 0%
where the time goes in v1:
time: 50 us; the launch traced here: 49.7 us
  Pallas kernels  41.5 us (83%)
  local copies, waits for them, and re-layouts  7.55 us (15%)
  between operations  0.64 us (1%)
    pallas_call x1, Pallas kernels, local(): pl.pallas_call(functools.partial(kernel, nvar, ngrp, norm), out_shape=(ja...  41.5 us
    unnamed x4, local copies, waits for them, and re-layouts  6.27 us
    broadcast_in_dim x1, local copies, waits for them, and re-layouts, local(): variant_weight[None, :]  1.28 us

profile of v1, /device:TPU:0, one launch (start us, length us, event | category | flops | bytes accessed | tf_op | source)
XLA Modules:
  0.0 49.7 jit_solution(8228873400996111238)
XLA Ops:
  0.6 1.3 %broadcast_in_dim.6.wt = bf16[1,1024]{1,0:T(2,128)(2,1)} reshape(bf16[1024]{0:T(1024)(128)(2,1)} %param.6) | data formatting | bytes 4096 | tf_op jit(solution)/shard_map/broadcast_in_dim | solution.py:262
  1.9 1.7 %copy.7.sw = bf16[1024,64]{1,0:T(8,128)(2,1)} copy(bf16[1024,64]{0,1:T(8,128)(2,1)} %param.8) | data formatting | bytes 262144 | tf_op args[3]
  3.6 1.7 %copy.8.lab = s32[512,64]{1,0:T(8,128)} copy(s32[512,64]{0,1:T(8,128)} %param.9) | data formatting | bytes 262144 | tf_op args[4]
  5.4 41.5 %shard_map.68 = (f32[128,64]{1,0:T(8,128)}, f32[1,1024]{1,0:T(1,128)}) custom-call(s32[4096,1024]{1,0:T(8,128)} %dos.1, bf16[1,1024]{1,0:T(2,128)(2,1)} %broadcast_in_dim.6.wt, s32[1,1024]{1,0:T(1,128)} %bitcast.3, bf16[1024,64]{1,0:T(8,128)(2,1)} %copy.7.sw, s32[512,64]{1,0:T(8,128)} %copy.8.lab), custom_call_target="tpu_custom_call" | custom-call | tf_op jit(solution)/shard_map/pallas_call | solution.py:219
  46.9 1.5 %copy.9 = f32[128,64]{0,1:T(8,128)} copy(f32[128,64]{1,0:T(8,128)} %get-tuple-element.6) | data formatting | bytes 65536
  48.5 1.3 %copy.11 = f32[1024]{0:T(1024)} copy(f32[1024]{0:T(1024)} %bitcast.2) | data formatting | bytes 8192

commit v2 on v1

--- a/solution.py
+++ b/solution.py
@@ -20,15 +20,14 @@
 
 
 def kernel(
-    nvar, ngrp, norm, dos, wt, bid, sw, lab, lev_out, wg_out,
-    dint, dose, wmat, bd, wown, labv, pred, part, own, yrecv, ysum, zrecv, gathz, gathy,
-    colacc, levacc, redl, redw,
+    nvar, ngrp, dos, wt_hbm, bid_hbm, sw, lab, redl, redw,
+    wt, bid, dint, dose, wmat, wback, wown, labv, pred, part, own, yrecv, ysum, zrecv, gathz, gathy,
+    colacc, levacc,
     dsem, csem, ys, yr, zs, zr, gzs, gzr, gys, gyr, rs, rr,
 ):
     nz = nvar // 2
-    rows = labv.shape[0]
-    half = rows // 2
-    kb, traits = wown.shape
+    rows = labv.shape[1]
+    traits, kb = wown.shape
     v = lax.axis_index("var")
     g = lax.axis_index("grp")
     z, y = v // 2, v % 2
@@ -41,8 +40,12 @@
         start = pl.multiple_of(b * rows, rows)
         return pltpu.make_async_copy(dos.at[pl.ds(start, rows)], dint.at[s], dsem.at[s])
 
-    sw_copy = pltpu.make_async_copy(sw.at[pl.ds(pl.multiple_of(v * kb, kb), kb)], wown, csem.at[0])
+    sw_copy = pltpu.make_async_copy(sw.at[:, pl.ds(pl.multiple_of(v * kb, kb), kb)], wown, csem.at[0])
     lab_copy = pltpu.make_async_copy(lab, labv, csem.at[1])
+    wt_copy = pltpu.make_async_copy(wt_hbm, wt, csem.at[2])
+    bid_copy = pltpu.make_async_copy(bid_hbm, bid, csem.at[3])
+    wt_copy.start()
+    bid_copy.start()
     sw_copy.start()
     for i in range(nz):
         dose_copy(i, block_of(i, 1 - y)).start()
@@ -57,13 +60,12 @@
     for d in range(1, ngrp):
         pl.semaphore_signal(barrier, inc=1, device_id={"grp": (g + d) % ngrp})
 
-    hot = lax.broadcasted_iota(jnp.int32, (kb, wt.shape[1]), 0) == bid[...]
-    wmat[...] = jnp.where(hot, wt[...].astype(F32), 0.0).T.astype(BF16)
+    wt_copy.wait()
+    bid_copy.wait()
+    hot = lax.broadcasted_iota(jnp.int32, (kb, wt.shape[0]), 0) == bid[...][None, :]
+    wmat[...] = jnp.where(hot, wt[...].astype(F32)[None, :], 0.0).T.astype(BF16)
     sw_copy.wait()
-    w = wown[...].astype(F32)
-    zero = jnp.zeros_like(w)
-    bd[0:kb, :] = jnp.concatenate([w, zero], axis=1).astype(BF16)
-    bd[kb : 2 * kb, :] = jnp.concatenate([zero, w], axis=1).astype(BF16)
+    wback[...] = wown[...].astype(F32).T.astype(BF16)
     colacc[...] = jnp.zeros_like(colacc)
     levacc[...] = jnp.zeros_like(levacc)
 
@@ -72,9 +74,10 @@
         d = dint[s].astype(F32).astype(BF16)
         dose[b] = d
         p = jnp.dot(d, wmat[...], preferred_element_type=F32).astype(BF16)
-        pp = jnp.concatenate([p[:half], p[half:]], axis=1)
-        pred[b] = pp
-        return jnp.dot(pp, bd[...], preferred_element_type=F32)
+        pred[b] = p
+        return lax.dot_general(
+            wown[...], p, (((1,), (1,)), ((), ())), preferred_element_type=F32
+        )
 
     def y_copy(i):
         return pltpu.make_async_remote_copy(
@@ -115,7 +118,6 @@
 
     lab_copy.wait()
     target = labv[...].astype(F32)
-    target = jnp.concatenate([target[:half], target[half:]], axis=1)
 
     for i in range(nz - 1):
         y_copy(i).wait_recv()
@@ -132,16 +134,9 @@
     gy_copy(nz - 1).start()
 
     def backward(resid, b):
-        lg = lax.dot_general(
-            resid, bd[...], (((1,), (1,)), ((), ())), preferred_element_type=F32
-        ).astype(BF16)
-        lg = jnp.concatenate([lg[:, :kb], lg[:, kb:]], axis=0)
-        colacc[...] += lax.dot_general(
-            lg, dose[b], (((0,), (0,)), ((), ())), preferred_element_type=F32
-        )
-        levacc[...] += lax.dot_general(
-            pred[b], resid, (((0,), (0,)), ((), ())), preferred_element_type=F32
-        )
+        lg = jnp.dot(wback[...], resid, preferred_element_type=F32).astype(BF16)
+        colacc[...] += jnp.dot(lg, dose[b], preferred_element_type=F32)
+        levacc[...] += jnp.dot(resid, pred[b], preferred_element_type=F32)
 
     backward(gathz[nz - 1], v)
     gy_copy(nz - 1).wait_recv()
@@ -162,10 +157,9 @@
 
     lax.fori_loop(0, nz - 1, gather_y, 0)
 
-    hot = lax.broadcasted_iota(jnp.int32, colacc.shape, 0) == bid[...]
+    hot = lax.broadcasted_iota(jnp.int32, colacc.shape, 0) == bid[...][None, :]
     redw[g] = jnp.sum(jnp.where(hot, colacc[...], 0.0), axis=0, keepdims=True)
-    lev = levacc[0:kb, 0:traits] + levacc[kb : 2 * kb, traits : 2 * traits]
-    redl[g] = jnp.concatenate([lev[: kb // 2], lev[kb // 2 :]], axis=1)
+    redl[g] = levacc[...]
 
     def r_copies(d):
         peer = {"grp": (g + d) % ngrp}
@@ -184,15 +178,6 @@
     for d in range(1, ngrp):
         for copy in r_copies(d):
             copy.wait_recv()
-    total, weight = redl[0], redw[0]
-    for e in range(1, ngrp):
-        total = total + redl[e]
-        weight = weight + redw[e]
-    total = total * norm
-    lev_out[0 : kb // 2, :] = total[:, :traits]
-    lev_out[kb // 2 : kb, :] = total[:, traits:]
-    wg_out[...] = weight * norm
-
     for i in range(nz):
         y_copy(i).wait_send()
         gy_copy(i).wait_send()
@@ -202,6 +187,15 @@
     for d in range(1, ngrp):
         for copy in r_copies(d):
             copy.wait_send()
+
+
+def add_groups(norm, redl, redw, lev_out, wg_out):
+    total, weight = redl[0], redw[0]
+    for e in range(1, redl.shape[0]):
+        total = total + redl[e]
+        weight = weight + redw[e]
+    lev_out[...] = total * norm
+    wg_out[...] = weight * norm
 
 
 def local(dosages, variant_weight, block_id, stack_weight, labels):
@@ -210,28 +204,30 @@
     total_preds, traits = stack_weight.shape
     kb = total_preds // nvar
     rows = labels.shape[0]
-    half, nz = rows // 2, nvar // 2
+    nz = nvar // 2
     norm = 1.0 / math.sqrt(persons * ngrp)
-    block = (half, 2 * traits)
+    block = (traits, rows)
     dma = pltpu.SemaphoreType.DMA
     hbm = pl.BlockSpec(memory_space=pl.ANY)
     vmem = pl.BlockSpec(memory_space=pltpu.VMEM)
-    level, weight = pl.pallas_call(
-        functools.partial(kernel, nvar, ngrp, norm),
+    sums = pl.pallas_call(
+        functools.partial(kernel, nvar, ngrp),
         out_shape=(
-            jax.ShapeDtypeStruct((kb, traits), F32),
-            jax.ShapeDtypeStruct((1, variants), F32),
+            jax.ShapeDtypeStruct((ngrp, traits, kb), F32),
+            jax.ShapeDtypeStruct((ngrp, 1, variants), F32),
         ),
-        in_specs=[hbm, vmem, vmem, hbm, hbm],
+        in_specs=[hbm] * 5,
         out_specs=(vmem, vmem),
         scratch_shapes=[
+            pltpu.VMEM((variants,), BF16),
+            pltpu.VMEM((variants,), jnp.int32),
             pltpu.VMEM((nvar, rows, variants), jnp.int32),
             pltpu.VMEM((nvar, rows, variants), BF16),
             pltpu.VMEM((variants, kb), BF16),
-            pltpu.VMEM((2 * kb, 2 * traits), BF16),
             pltpu.VMEM((kb, traits), BF16),
-            pltpu.VMEM((rows, traits), jnp.int32),
-            pltpu.VMEM((nvar, half, 2 * kb), BF16),
+            pltpu.VMEM((traits, kb), BF16),
+            pltpu.VMEM((traits, rows), jnp.int32),
+            pltpu.VMEM((nvar, rows, kb), BF16),
             pltpu.VMEM((nz,) + block, F32),
             pltpu.VMEM((nz,) + block, F32),
             pltpu.VMEM((nz,) + block, F32),
@@ -240,11 +236,9 @@
             pltpu.VMEM((nz,) + block, BF16),
             pltpu.VMEM((nz,) + block, BF16),
             pltpu.VMEM((kb, variants), F32),
-            pltpu.VMEM((2 * kb, 2 * traits), F32),
-            pltpu.VMEM((ngrp, kb // 2, 2 * traits), F32),
-            pltpu.VMEM((ngrp, 1, variants), F32),
+            pltpu.VMEM((traits, kb), F32),
             dma((nvar,)),
-            dma((2,)),
+            dma((4,)),
             dma((nz,)),
             dma((nz,)),
             dma((nz,)),
@@ -259,8 +253,17 @@
         compiler_params=pltpu.CompilerParams(
             collective_id=0, has_side_effects=True, vmem_limit_bytes=60 * 1024 * 1024
         ),
-    )(dosages, variant_weight[None, :], block_id[None, :], stack_weight, labels)
-    return level, weight.reshape(variants)
+    )(dosages, variant_weight, block_id, stack_weight.T, labels.T)
+    level, weight = pl.pallas_call(
+        functools.partial(add_groups, norm),
+        out_shape=(
+            jax.ShapeDtypeStruct((traits, kb), F32),
+            jax.ShapeDtypeStruct((1, variants), F32),
+        ),
+        in_specs=[vmem, vmem],
+        out_specs=(vmem, vmem),
+    )(*sums)
+    return level.T, weight.reshape(variants)
 
 
 def solution(mesh):

time: 50 us -> 43.3 us (0.87)
  local copies, waits for them, and re-layouts: 7.55 us -> 0 us
  Pallas kernels: 41.5 us -> 42.6 us
    unnamed x4 -> x0, local copies, waits for them, and re-layouts: 6.27 us -> none
    broadcast_in_dim x1 -> x0, local copies, waits for them, and re-layouts: 1.28 us -> none  [local(): variant_weight[None, :]]
    pallas_call x1 -> x2, Pallas kernels: 41.5 us -> 42.6 us  [the longest x1 41 us: local(): pl.pallas_call(functools.partial(kernel, nvar, ngrp), out_shape=(jax.Shap...]
where the time goes in v2:
time: 43.3 us; the launch traced here: 43.2 us
  Pallas kernels  42.6 us (98%)
  between operations  0.64 us (1%)
    pallas_call x1, Pallas kernels, local(): pl.pallas_call(functools.partial(kernel, nvar, ngrp), out_shape=(jax.Shap...  41 us
    pallas_call x1, Pallas kernels, local(): pl.pallas_call(functools.partial(add_groups, norm), out_shape=(jax.ShapeD...  1.53 us

profile of v2, /device:TPU:0, one launch (start us, length us, event | category | flops | bytes accessed | tf_op | source)
XLA Modules:
  0.0 43.2 jit_solution(637345326065566582)
XLA Ops:
  0.6 41.0 %shard_map.68 = (f32[4,64,128]{2,1,0:T(8,128)}, f32[4,1,1024]{2,1,0:T(1,128)}) custom-call(s32[4096,1024]{1,0:T(8,128)} %dos.1, bf16[1024]{0:T(1024)(128)(2,1)} %wt_hbm.1, s32[1024]{0:T(1024)} %bid_hbm.1, bf16[64,1024]{1,0:T(8,128)(2,1)} %bitcast.4, s32[64,512]{1,0:T(8,128)} %bitcast.5), custom_call_target="tpu_custom_call" | custom-call | tf_op jit(solution)/shard_map/pallas_call | solution.py:213
  41.7 1.5 %shard_map.69 = (f32[64,128]{1,0:T(8,128)}, f32[1,1024]{1,0:T(1,128)}) custom-call(f32[4,64,128]{2,1,0:T(8,128)} %get-tuple-element.6.redl, f32[4,1,1024]{2,1,0:T(1,128)} %get-tuple-element.7.redw), custom_call_target="tpu_custom_call" | custom-call | tf_op jit(solution)/shard_map/pallas_call | solution.py:257

commit v3 on v2

v3 whole, which is shorter than its diff:
```python
import functools
import math

import jax
import jax.numpy as jnp
from jax import lax
from jax.experimental import pallas as pl
from jax.experimental.pallas import tpu as pltpu
from jax.sharding import PartitionSpec as P

F32, BF16 = jnp.float32, jnp.bfloat16


def flip(a, k, count):
    total, bit = 0, 1
    while bit < count:
        total = total + bit * ((a // bit + k // bit) % 2)
        bit *= 2
    return total


def zeros_below(k, bits):
    count = 0
    while count < bits and k % (1 << (count + 1)) == 0:
        count += 1
    return count


def kernel(
    nvar, ngrp, cuts, window, dos, wt_hbm, bid_hbm, sw, lab, redl, redw,
    wt, bid, dint, dose, wmat, wback, wown, labv, pred, part, own, yrecv, zrecv, gathz, gathy,
    colacc, levacc,
    dsem, csem, ys, yr, zs, zr, gzs, gzr, gys, gyr, rs, rr,
):
    nz = nvar // 2
    bits = nz.bit_length() - 1
    half = cuts * nz
    traits, sub = part.shape[1:]
    kb = wown.shape[1]
    v = lax.axis_index("var")
    g = lax.axis_index("grp")
    z, y = v // 2, v % 2
    partner = z * 2 + (1 - y)

    def piece(k, parity, h):
        return (flip(z, k, nz) * 2 + parity) * cuts + h

    def place(s):
        late = s // half
        q, t = s, s - half
        h = (1 - late) * (q // nz) + late * (t % cuts)
        i = (1 - late) * (q % nz) + late * (t // cuts)
        return piece(nz - 1 - i, y * late + (1 - y) * (1 - late), h)

    def dose_copy(s):
        start = pl.multiple_of(place(s) * sub, sub)
        return pltpu.make_async_copy(dos.at[pl.ds(start, sub)], dint.at[s], dsem.at[s])

    wt_copy = pltpu.make_async_copy(wt_hbm, wt, csem.at[2])
    bid_copy = pltpu.make_async_copy(bid_hbm, bid, csem.at[3])
    sw_copy = pltpu.make_async_copy(
        sw.at[:, pl.ds(pl.multiple_of(v * kb, kb), kb)], wown, csem.at[0]
    )
    lab_copy = pltpu.make_async_copy(lab, labv, csem.at[1])
    wt_copy.start()
    bid_copy.start()
    sw_copy.start()
    for s in range(window):
        dose_copy(s).start()
    lab_copy.start()

    barrier = pltpu.get_barrier_semaphore()
    pl.semaphore_signal(barrier, inc=1, device_id={"var": partner})
    for r in range(bits):
        pl.semaphore_signal(barrier, inc=1, device_id={"var": flip(z, 1 << r, nz) * 2 + y})
    for d in range(1, ngrp):
        pl.semaphore_signal(barrier, inc=1, device_id={"grp": (g + d) % ngrp})

    wt_copy.wait()
    bid_copy.wait()
    hot = lax.broadcasted_iota(jnp.int32, (kb, wt.shape[0]), 0) == bid[...][None, :]
    wmat[...] = jnp.where(hot, wt[...].astype(F32)[None, :], 0.0).T.astype(BF16)
    sw_copy.wait()
    wback[...] = wown[...].astype(F32).T.astype(BF16)
    colacc[...] = jnp.zeros_like(colacc)
    levacc[...] = jnp.zeros_like(levacc)

    def forward(s):
        dose_copy(s).wait()
        ahead = s + window
        if isinstance(s, int):
            if ahead < 2 * half:
                dose_copy(ahead).start()
        else:

            @pl.when(ahead < 2 * half)
            def _():
                dose_copy(ahead).start()

        at = place(s)
        d = dint[s].astype(F32).astype(BF16)
        dose[at] = d
        p = jnp.dot(d, wmat[...], preferred_element_type=F32).astype(BF16)
        pred[at] = p
        return lax.dot_general(
            wown[...], p, (((1,), (1,)), ((), ())), preferred_element_type=F32
        )

    def remote(src, dst, send, recv, peer):
        return pltpu.make_async_remote_copy(src, dst, send, recv, device_id={"var": peer})

    def across(r):
        return flip(z, 1 << r, nz) * 2 + y

    def y_copy(q):
        return remote(part.at[q], yrecv.at[q], ys.at[q], yr.at[q], partner)

    def z_copy(h, k):
        q = h * nz + nz - 1 - k
        peer = across(zeros_below(k, bits))
        return remote(own.at[q], zrecv.at[q], zs.at[q], zr.at[q], peer)

    def gz_copy(h, k):
        r = zeros_below(k, bits)
        q, src = h * nz + k, h * nz + k - (1 << r)
        return remote(gathz.at[src], gathz.at[q], gzs.at[q], gzr.at[q], across(r))

    def gy_copy(q):
        return remote(gathz.at[q], gathy.at[q], gys.at[q], gyr.at[q], partner)

    part[0] = forward(0)
    pl.semaphore_wait(barrier, bits + ngrp)
    y_copy(0).start()

    def first(s, carry):
        part[s] = forward(s)
        y_copy(s).start()
        return carry

    lax.fori_loop(1, half, first, 0)

    def reduce_step(h, k):
        q = h * nz + nz - 1 - k
        y_copy(q).wait_recv()
        total = own[q] + yrecv[q]
        for r in range(zeros_below(k, bits) if k else bits):
            other = k + (1 << r)
            z_copy(h, other).wait_recv()
            total = total + zrecv[h * nz + nz - 1 - other]
        if k:
            own[q] = total
            z_copy(h, k).start()
            return
        target = labv[:, h * sub : (h + 1) * sub].astype(F32)
        gathz[h * nz] = (jax.nn.sigmoid(total) - target).astype(BF16)
        send_on(h, 0)

    def send_on(h, k):
        for r in reversed(range(zeros_below(k, bits) if k else bits)):
            gz_copy(h, k + (1 << r)).start()
        gy_copy(h * nz + k).start()

    def backward(resid, at):
        lg = jnp.dot(wback[...], resid, preferred_element_type=F32).astype(BF16)
        colacc[...] += jnp.dot(lg, dose[at], preferred_element_type=F32)
        levacc[...] += jnp.dot(resid, pred[at], preferred_element_type=F32)

    def gather_step(h, k):
        gz_copy(h, k).wait_recv()
        send_on(h, k)

    order = sorted(range(1, nz), key=lambda k: (-zeros_below(k, bits), k))

    lab_copy.wait()
    for i in range(nz):
        for h in range(cuts):
            own[h * nz + i] = forward(half + i * cuts + h)
        if i < nz - 1:
            reduce_step(0, nz - 1 - i)
    for h in range(cuts):
        if h + 1 < cuts:
            reduce_step(h + 1, nz - 1)
        reduce_step(h, 0)
        if h + 1 < cuts:
            for k in range(nz - 2, 0, -1):
                reduce_step(h + 1, k)
        else:
            for k in order:
                gather_step(h, k)
        if h + 1 < cuts:
            for k in order:
                gather_step(h, k)

    def near(q, carry):
        backward(gathz[q], piece(q % nz, y, q // nz))
        return carry

    def far(q, carry):
        gy_copy(q).wait_recv()
        backward(gathy[q], piece(q % nz, 1 - y, q // nz))
        return carry

    for h in range(cuts):
        lax.fori_loop(h * nz, (h + 1) * nz, near, 0)
        lax.fori_loop(h * nz, (h + 1) * nz, far, 0)

    hot = lax.broadcasted_iota(jnp.int32, colacc.shape, 0) == bid[...][None, :]
    redw[g] = jnp.sum(jnp.where(hot, colacc[...], 0.0), axis=0, keepdims=True)
    redl[g] = levacc[...]

    def r_copies(d):
        peer = {"grp": (g + d) % ngrp}
        return (
            pltpu.make_async_remote_copy(
                redl.at[g], redl.at[g], rs.at[0, d - 1], rr.at[0, d - 1], device_id=peer
            ),
            pltpu.make_async_remote_copy(
                redw.at[g], redw.at[g], rs.at[1, d - 1], rr.at[1, d - 1], device_id=peer
            ),
        )

    for d in range(1, ngrp):
        for copy in r_copies(d):
            copy.start()
    for h in range(cuts):
        for k in range(nz):
            y_copy(h * nz + k).wait_send()
            gy_copy(h * nz + k).wait_send()
            if k:
                z_copy(h, k).wait_send()
                gz_copy(h, k).wait_send()
    for d in range(1, ngrp):
        for copy in r_copies(d):
            copy.wait_send()
            copy.wait_recv()


def add_groups(norm, redl, redw, lev_out, wg_out):
    total, weight = redl[0], redw[0]
    for e in range(1, redl.shape[0]):
        total = total + redl[e]
        weight = weight + redw[e]
    lev_out[...] = total * norm
    wg_out[...] = weight * norm


def local(dosages, variant_weight, block_id, stack_weight, labels):
    persons, variants = dosages.shape
    nvar, ngrp = lax.axis_size("var"), lax.axis_size("grp")
    total_preds, traits = stack_weight.shape
    kb = total_preds // nvar
    rows = labels.shape[0]
    cuts = 2 if rows % 256 == 0 else 1
    sub, count = rows // cuts, cuts * nvar // 2
    norm = 1.0 / math.sqrt(persons * ngrp)
    block = (count, traits, sub)
    dma = pltpu.SemaphoreType.DMA
    hbm = pl.BlockSpec(memory_space=pl.ANY)
    vmem = pl.BlockSpec(memory_space=pltpu.VMEM)
    sums = pl.pallas_call(
        functools.partial(kernel, nvar, ngrp, cuts, min(6, cuts * nvar)),
        out_shape=(
            jax.ShapeDtypeStruct((ngrp, traits, kb), F32),
            jax.ShapeDtypeStruct((ngrp, 1, variants), F32),
        ),
        in_specs=[hbm] * 5,
        out_specs=(vmem, vmem),
        scratch_shapes=[
            pltpu.VMEM((variants,), BF16),
            pltpu.VMEM((variants,), jnp.int32),
            pltpu.VMEM((2 * count, sub, variants), jnp.int32),
            pltpu.VMEM((2 * count, sub, variants), BF16),
            pltpu.VMEM((variants, kb), BF16),
            pltpu.VMEM((kb, traits), BF16),
            pltpu.VMEM((traits, kb), BF16),
            pltpu.VMEM((traits, rows), jnp.int32),
            pltpu.VMEM((2 * count, sub, kb), BF16),
            pltpu.VMEM(block, F32),
            pltpu.VMEM(block, F32),
            pltpu.VMEM(block, F32),
            pltpu.VMEM(block, F32),
            pltpu.VMEM(block, BF16),
            pltpu.VMEM(block, BF16),
            pltpu.VMEM((kb, variants), F32),
            pltpu.VMEM((traits, kb), F32),
            dma((2 * count,)),
            dma((4,)),
            dma((count,)),
            dma((count,)),
            dma((count,)),
            dma((count,)),
            dma((count,)),
            dma((count,)),
            dma((count,)),
            dma((count,)),
            dma((2, ngrp - 1)),
            dma((2, ngrp - 1)),
        ],
        compiler_params=pltpu.CompilerParams(
            collective_id=0, has_side_effects=True, vmem_limit_bytes=60 * 1024 * 1024
        ),
    )(dosages, variant_weight, block_id, stack_weight.T, labels.T)
    level, weight = pl.pallas_call(
        functools.partial(add_groups, norm),
        out_shape=(
            jax.ShapeDtypeStruct((traits, kb), F32),
            jax.ShapeDtypeStruct((1, variants), F32),
        ),
        in_specs=[vmem, vmem],
        out_specs=(vmem, vmem),
    )(*sums)
    return level.T, weight.reshape(variants)


def solution(mesh):
    return jax.shard_map(
        local,
        mesh=mesh,
        in_specs=(P("grp", "var"), P("var"), P("var"), P(), P(("grp", "var"), None)),
        out_specs=(P("var", None), P("var")),
        check_vma=False,
    )
```

time: 43.3 us -> 43.8 us (1.012)
    pallas_call x1, Pallas kernels: 41 us -> 41.5 us  [local(): pl.pallas_call(functools.partial(kernel, nvar, ngrp, cuts, min(6, cuts *...]
where the time goes in v3:
time: 43.8 us; the launch traced here: 43.6 us
  Pallas kernels  43 us (98%)
  between operations  0.64 us (1%)
    pallas_call x1, Pallas kernels, local(): pl.pallas_call(functools.partial(kernel, nvar, ngrp, cuts, min(6, cuts *...  41.5 us
    pallas_call x1, Pallas kernels, local(): pl.pallas_call(functools.partial(add_groups, norm), out_shape=(jax.ShapeD...  1.53 us

profile of v3, /device:TPU:0, one launch (start us, length us, event | category | flops | bytes accessed | tf_op | source)
XLA Modules:
  0.0 43.6 jit_solution(14019945976867259234)
XLA Ops:
  0.6 41.5 %shard_map.68 = (f32[4,64,128]{2,1,0:T(8,128)}, f32[4,1,1024]{2,1,0:T(1,128)}) custom-call(s32[4096,1024]{1,0:T(8,128)} %dos.1, bf16[1024]{0:T(1024)(128)(2,1)} %wt_hbm.1, s32[1024]{0:T(1024)} %bid_hbm.1, bf16[64,1024]{1,0:T(8,128)(2,1)} %bitcast.4, s32[64,512]{1,0:T(8,128)} %bitcast.5), custom_call_target="tpu_custom_call" | custom-call | tf_op jit(solution)/shard_map/pallas_call | solution.py:260
  42.1 1.5 %shard_map.69 = (f32[64,128]{1,0:T(8,128)}, f32[1,1024]{1,0:T(1,128)}) custom-call(f32[4,64,128]{2,1,0:T(8,128)} %get-tuple-element.6.redl, f32[4,1,1024]{2,1,0:T(1,128)} %get-tuple-element.7.redw), custom_call_target="tpu_custom_call" | custom-call | tf_op jit(solution)/shard_map/pallas_call | solution.py:303

commit v4 on v3

--- a/solution.py
+++ b/solution.py
@@ -35,6 +35,7 @@
     nz = nvar // 2
     bits = nz.bit_length() - 1
     half = cuts * nz
+    flight = 2
     traits, sub = part.shape[1:]
     kb = wown.shape[1]
     v = lax.axis_index("var")
@@ -134,14 +135,22 @@
 
     def first(s, carry):
         part[s] = forward(s)
-        y_copy(s).start()
+
+        @pl.when(s < flight)
+        def _():
+            y_copy(s).start()
+
         return carry
 
     lax.fori_loop(1, half, first, 0)
+    started = [min(flight, half)]
 
     def reduce_step(h, k):
         q = h * nz + nz - 1 - k
         y_copy(q).wait_recv()
+        if started[0] < half:
+            y_copy(started[0]).start()
+            started[0] += 1
         total = own[q] + yrecv[q]
         for r in range(zeros_below(k, bits) if k else bits):
             other = k + (1 << r)
@@ -168,6 +177,15 @@
     def gather_step(h, k):
         gz_copy(h, k).wait_recv()
         send_on(h, k)
+
+    def near(q, carry):
+        backward(gathz[q], piece(q % nz, y, q // nz))
+        return carry
+
+    def far(q, carry):
+        gy_copy(q).wait_recv()
+        backward(gathy[q], piece(q % nz, 1 - y, q // nz))
+        return carry
 
     order = sorted(range(1, nz), key=lambda k: (-zeros_below(k, bits), k))
 
@@ -184,25 +202,17 @@
         if h + 1 < cuts:
             for k in range(nz - 2, 0, -1):
                 reduce_step(h + 1, k)
-        else:
             for k in order:
                 gather_step(h, k)
-        if h + 1 < cuts:
+        else:
+            if h:
+                lax.fori_loop(0, h * nz, near, 0)
             for k in order:
                 gather_step(h, k)
-
-    def near(q, carry):
-        backward(gathz[q], piece(q % nz, y, q // nz))
-        return carry
-
-    def far(q, carry):
-        gy_copy(q).wait_recv()
-        backward(gathy[q], piece(q % nz, 1 - y, q // nz))
-        return carry
-
-    for h in range(cuts):
-        lax.fori_loop(h * nz, (h + 1) * nz, near, 0)
-        lax.fori_loop(h * nz, (h + 1) * nz, far, 0)
+    if cuts > 1:
+        lax.fori_loop(0, half - nz, far, 0)
+    lax.fori_loop(half - nz, half, near, 0)
+    lax.fori_loop(half - nz, half, far, 0)
 
     hot = lax.broadcasted_iota(jnp.int32, colacc.shape, 0) == bid[...][None, :]
     redw[g] = jnp.sum(jnp.where(hot, colacc[...], 0.0), axis=0, keepdims=True)
@@ -250,7 +260,7 @@
     total_preds, traits = stack_weight.shape
     kb = total_preds // nvar
     rows = labels.shape[0]
-    cuts = 2 if rows % 256 == 0 else 1
+    cuts = 1
     sub, count = rows // cuts, cuts * nvar // 2
     norm = 1.0 / math.sqrt(persons * ngrp)
     block = (count, traits, sub)
@@ -258,7 +268,7 @@
     hbm = pl.BlockSpec(memory_space=pl.ANY)
     vmem = pl.BlockSpec(memory_space=pltpu.VMEM)
     sums = pl.pallas_call(
-        functools.partial(kernel, nvar, ngrp, cuts, min(6, cuts * nvar)),
+        functools.partial(kernel, nvar, ngrp, cuts, min(3, cuts * nvar)),
         out_shape=(
             jax.ShapeDtypeStruct((ngrp, traits, kb), F32),
             jax.ShapeDtypeStruct((ngrp, 1, variants), F32),

time: 43.8 us -> 40.4 us (0.922)
  Pallas kernels: 43 us -> 39.6 us
    pallas_call x1, Pallas kernels: 41.5 us -> 38.1 us  [local(): pl.pallas_call(functools.partial(kernel, nvar, ngrp, cuts, min(3, cuts *...]
where the time goes in v4:
time: 40.4 us; the launch traced here: 40.2 us
  Pallas kernels  39.6 us (98%)
  between operations  0.64 us (2%)
    pallas_call x1, Pallas kernels, local(): pl.pallas_call(functools.partial(kernel, nvar, ngrp, cuts, min(3, cuts *...  38.1 us
    pallas_call x1, Pallas kernels, local(): pl.pallas_call(functools.partial(add_groups, norm), out_shape=(jax.ShapeD...  1.53 us

profile of v4, /device:TPU:0, one launch (start us, length us, event | category | flops | bytes accessed | tf_op | source)
XLA Modules:
  0.0 40.2 jit_solution(6776516006378921025)
XLA Ops:
  0.6 38.1 %shard_map.68 = (f32[4,64,128]{2,1,0:T(8,128)}, f32[4,1,1024]{2,1,0:T(1,128)}) custom-call(s32[4096,1024]{1,0:T(8,128)} %dos.1, bf16[1024]{0:T(1024)(128)(2,1)} %wt_hbm.1, s32[1024]{0:T(1024)} %bid_hbm.1, bf16[64,1024]{1,0:T(8,128)(2,1)} %bitcast.4, s32[64,512]{1,0:T(8,128)} %bitcast.5), custom_call_target="tpu_custom_call" | custom-call | tf_op jit(solution)/shard_map/pallas_call | solution.py:270
  38.7 1.5 %shard_map.69 = (f32[64,128]{1,0:T(8,128)}, f32[1,1024]{1,0:T(1,128)}) custom-call(f32[4,64,128]{2,1,0:T(8,128)} %get-tuple-element.6.redl, f32[4,1,1024]{2,1,0:T(1,128)} %get-tuple-element.7.redw), custom_call_target="tpu_custom_call" | custom-call | tf_op jit(solution)/shard_map/pallas_call | solution.py:313
